TPU v7x, 512 devices: a whole 4x8x8 slice. The times are simulated.
512 devices in a mesh: mod: 2 (over z_hi), loop: 16 (over x, z_lo), line: 16 (over y, core).
Axes of the slice: x: 4, y: 8, z: 8 (z_hi: 2, z_lo: 4; z = z_hi * 4 + z_lo), core: 2. Of those that a mesh axis runs over, the one named last changes fastest.
Arguments:
- act: bfloat16 [2, 196608, 512], P('mod', ('loop', 'line'))
- dy: bfloat16 [2, 196608, 1280], P('mod', ('loop', 'line')), may hold values from -6 to 6
- w_out: bfloat16 [2, 512, 1280], P('mod'), may hold values from -0.15625 to 0.15625
- counts: int32 [2, 16, 16], P('mod', 'loop', 'line'), may hold values from 192 to 768, as said below
Outputs:
- grad_clipped: float32 [2, 512, 1280], P('mod', 'loop')
- hidden_grad: bfloat16 [2, 196608, 512], P('mod', ('loop', 'line'))
Inputs may be any that keep to these rules, and one draw needn't show every extreme that they name: `counts`: in each tower some device has all 768 slots live.
All inputs are finite; a program needn't handle non-finite values.
Results may differ from a plain program's by a relative error of at most 0.001.
Values sent between devices are 32-bit elements; how exact they have to be, the bound alone decides.
A program may use at most 64 MiB of HBM per device.

v0:
```python
import jax
import jax.numpy as jnp
from jax import lax
from jax.sharding import PartitionSpec as P


def on_device(act, dy, w_out, counts):
    tokens = act[0]
    upstream = dy[0]
    weight = w_out[0]
    rows = tokens.shape[0]
    hidden = tokens.shape[1]
    block = weight.shape[1]
    live = lax.broadcasted_iota(jnp.int32, (rows, 1), 0) < counts[0, 0]
    masked = jnp.where(live, tokens, jnp.zeros_like(tokens))
    entries = lax.axis_size("mod") * hidden * block
    share = lax.psum_scatter(
        lax.dot_general(
            masked, upstream, (((0,), (0,)), ((), ())), preferred_element_type=jnp.float32
        ),
        "loop",
        scatter_dimension=0,
        tiled=True,
    )
    share = lax.psum(share, "line")
    total = lax.psum(jnp.sum(share * share), ("mod", "loop"))
    factor = 1.0 / jnp.sqrt(total / entries + 1e-06)
    clipped = share * factor
    back = lax.dot_general(
        upstream, weight, (((1,), (1,)), ((), ())), preferred_element_type=jnp.float32
    )
    hidden_grad = jnp.where(live, back, jnp.zeros_like(back)).astype(jnp.bfloat16)
    return (clipped[None], hidden_grad[None])


def solution(mesh):
    in_specs = (
        P("mod", ("loop", "line"), None),
        P("mod", ("loop", "line"), None),
        P("mod", None, None),
        P("mod", "loop", "line"),
    )
    out_specs = (P("mod", "loop", None), P("mod", ("loop", "line"), None))
    return jax.shard_map(
        on_device, mesh=mesh, in_specs=in_specs, out_specs=out_specs, check_vma=False
    )
```

profile of v0, /device:TPU:8, one launch (start us, length us, event | category | flops | bytes accessed | tf_op | source)
XLA Modules:
  0.0 310.6 jit_solution(13326542029925265666)
XLA Ops:
  7.2 0.0 copy-start
  7.2 0.0 reduce-scatter.2.cloned.1.call-start
  8.0 0.7 copy-done
  8.7 3.9 %fusion.2 = f32[512,1280]{1,0:T(8,128)} fusion(bf16[1,768,1280]{2,1,0:T(8,128)(2,1)S(1)} %copy-done, bf16[1,768,512]{2,1,0:T(8,128)(2,1)} %param.4, pred[768]{0:T(1024)(128)(4,1)S(1)} %iota_compare_fusion), kind=kOutput, calls=%fused_computation.2 | convolution fusion | flops 1007026176 | bytes 5374720 | tf_op jit(solution)/shard_map/dot_general | solution.py:18
  12.7 0.0 copy-start.2
  12.7 0.0 reduce-scatter.2.cloned.1.call-update
  12.7 0.0 all-reduce.2.cloned.1.call-start
  12.8 101.7 %reduce-scatter.2.cloned.1.call-done = f32[32,1280]{1,0:T(8,128)} async-done(((f32[512,1280]{1,0:T(8,128)}), f32[32,1280]{1,0:T(8,128)}) %reduce-scatter.2.cloned.1.call-update) | async-done | bytes 163856 | tf_op jit(solution)/shard_map/reduce_scatter | solution.py:17
  114.5 0.0 all-reduce.2.cloned.1.call-update
  114.5 108.3 %all-reduce.2.cloned.1.call-done = f32[32,1280]{1,0:T(8,128)} async-done(((f32[32,1280]{1,0:T(8,128)}), f32[32,1280]{1,0:T(8,128)}) %all-reduce.2.cloned.1.call-update) | async-done | bytes 163856 | tf_op jit(solution)/shard_map/psum | solution.py:25
  222.8 1.6 multiply_reduce_fusion
  224.4 0.0 copy-done.2
  224.4 0.0 copy-start.1
  224.4 2.1 fusion.7
  226.5 75.9 %psum.15 = f32[]{:T(128)} all-reduce(f32[]{:T(128)} %multiply_reduce_fusion), channel_id=1, replica_groups=mesh['mod'=2,'loop'=16,'line'=16] {'mod','loop'}, use_global_device_ids=true, to_apply=%region_3.4 | all-reduce | flops 1 | bytes 8 | tf_op jit(solution)/shard_map/psum | solution.py:26
  303.1 0.0 copy-done.1
  303.1 0.7 multiply_bitcast_fusion
  (1 shorter events, 0.0 us)
Async XLA Ops:
  7.2 1.6 copy-start
  7.2 107.3 %reduce-scatter.2.cloned.1.call-start = ((), (), s32[]{:S(2)}) async-start(), calls=%async_computation.1 | async-start | bytes 2785280 | tf_op jit(solution)/shard_map/reduce_scatter | solution.py:17
  12.7 211.7 %copy-start.2 = (bf16[1,512,1280]{2,1,0:T(8,128)(2,1)S(1)}, bf16[1,512,1280]{2,1,0:T(8,128)(2,1)}, u32[]{:S(2)}) copy-start(bf16[1,512,1280]{2,1,0:T(8,128)(2,1)} %param.6) | copy-start | bytes 3932164
  12.7 210.1 %all-reduce.2.cloned.1.call-start = ((), (), s32[]{:S(2)}) async-start(), calls=%async_computation.2 | async-start | bytes 327680 | tf_op jit(solution)/shard_map/psum | solution.py:25
  224.4 78.7 %copy-start.1 = (f32[32,1280]{1,0:T(8,128)S(1)}, f32[32,1280]{1,0:T(8,128)}, u32[]{:S(2)}) copy-start(f32[32,1280]{1,0:T(8,128)} %all-reduce.2.cloned.1.call-done) | copy-start | bytes 491524
Sparse Core Ops, SparseCore 0:
  12.8 101.6 reduce-scatter.1
  116.8 105.9 all-reduce.1
where the time goes:
time: 311 us
  waiting for transfers between devices  210 us (68%)
  blocking collectives  75.9 us (24%)
  between operations  15.5 us (5%)
  matrix products  6.04 us (2%)
    psum x1, waiting for transfers between devices, on_device(): share = lax.psum(share, 'line')  108 us
    reduce_scatter x1, waiting for transfers between devices, on_device(): lax.psum_scatter(lax.dot_general(masked, upstream, (((0,), (0,)), ((), ()...  102 us
    psum x1, blocking collectives, on_device(): total = lax.psum(jnp.sum(share * share), ('mod', 'loop'))  75.9 us
  transfers between devices with their start and end apart: 2, of which 2 were waited for; matrix products, arithmetic and copies ran while one was open for 0% of the time, Pallas kernels for 0%

commit v1 on v0

--- a/solution.py
+++ b/solution.py
@@ -22,7 +22,9 @@
         scatter_dimension=0,
         tiled=True,
     )
-    share = lax.psum(share, "line")
+    share = share
+    for hop in (1, 2, 4, 8):
+        share = share + lax.ppermute(share, "line", [(dev, dev ^ hop) for dev in range(16)])
     total = lax.psum(jnp.sum(share * share), ("mod", "loop"))
     factor = 1.0 / jnp.sqrt(total / entries + 1e-06)
     clipped = share * factor

time: 311 us -> 236 us (0.76)
  the two profiles are of different devices: /device:TPU:8 before, /device:TPU:56 now
where the time goes in v1:
time: 236 us
  waiting for transfers between devices  123 us (52%)
  blocking collectives  74.1 us (31%)
  between operations  15.6 us (7%)
  starting transfers between devices  14.4 us (6%)
  matrix products  6.05 us (3%)
    reduce_scatter x1, waiting for transfers between devices, on_device(): lax.psum_scatter(lax.dot_general(masked, upstream, (((0,), (0,)), ((), ()...  101 us
    psum x1, blocking collectives, on_device(): total = lax.psum(jnp.sum(share * share), ('mod', 'loop'))  74.1 us
    ppermute x4, waiting for transfers between devices, on_device(): lax.ppermute(share, 'line', [(dev, dev ^ hop) for dev in range(16)])  21.6 us
    ppermute x4, starting transfers between devices, on_device(): lax.ppermute(share, 'line', [(dev, dev ^ hop) for dev in range(16)])  14.4 us
  transfers between devices with their start and end apart: 5, of which 5 were waited for; matrix products, arithmetic and copies ran while one was open for 1% of the time, Pallas kernels for 0%

profile of v1, /device:TPU:56, one launch (start us, length us, event | category | flops | bytes accessed | tf_op | source)
XLA Modules:
  0.0 235.7 jit_solution(17020692300539463405)
XLA Ops:
  7.2 0.0 copy-start
  7.2 0.0 reduce-scatter.2.cloned.1.call-start
  8.0 0.7 copy-done
  8.7 4.0 %fusion.2 = f32[512,1280]{1,0:T(8,128)} fusion(bf16[1,768,1280]{2,1,0:T(8,128)(2,1)S(1)} %copy-done, bf16[1,768,512]{2,1,0:T(8,128)(2,1)} %param.4, pred[768]{0:T(1024)(128)(4,1)S(1)} %iota_compare_fusion), kind=kOutput, calls=%fused_computation.2 | convolution fusion | flops 1007026176 | bytes 5374720 | tf_op jit(solution)/shard_map/dot_general | solution.py:18
  12.7 0.0 copy-start.1
  12.7 0.0 reduce-scatter.2.cloned.1.call-update
  12.7 100.9 %reduce-scatter.2.cloned.1.call-done = f32[32,1280]{1,0:T(8,128)} async-done(((f32[512,1280]{1,0:T(8,128)}), f32[32,1280]{1,0:T(8,128)}) %reduce-scatter.2.cloned.1.call-update) | async-done | bytes 163856 | tf_op jit(solution)/shard_map/reduce_scatter | solution.py:17
  113.7 1.9 collective-permute-start
  115.6 1.6 collective-permute-done
  117.1 0.9 add.19
  118.1 3.2 %collective-permute-start.1 = (f32[32,1280]{1,0:T(8,128)S(1)}, f32[32,1280]{1,0:T(8,128)S(1)}, u32[]{:S(2)}, u32[]{:S(2)}) collective-permute-start(f32[32,1280]{1,0:T(8,128)S(1)} %add.19), channel_id=1, source_target_pairs={{0,2},{1,3},{2,0},{3,1},{4,6},{5,7},{6,4},{7,5},{8,10},{9,11},{10,... | collective-permute-start | bytes 491528 | tf_op jit(solution)/shard_map/ppermute | solution.py:27
  121.3 4.9 %collective-permute-done.1 = f32[32,1280]{1,0:T(8,128)S(1)} collective-permute-done((f32[32,1280]{1,0:T(8,128)S(1)}, f32[32,1280]{1,0:T(8,128)S(1)}, u32[]{:S(2)}, u32[]{:S(2)}) %collective-permute-start.1) | collective-permute-done | bytes 163872 | tf_op jit(solution)/shard_map/ppermute | solution.py:27
  126.3 4.5 %collective-permute-start.2 = (f32[32,1280]{1,0:T(8,128)S(1)}, f32[32,1280]{1,0:T(8,128)S(1)}, u32[]{:S(2)}, u32[]{:S(2)}) collective-permute-start(f32[32,1280]{1,0:T(8,128)S(1)} %add.20), channel_id=1, source_target_pairs={{0,4},{1,5},{2,6},{3,7},{4,0},{5,1},{6,2},{7,3},{8,12},{9,13},{10,... | collective-permute-start | bytes 491528 | tf_op jit(solution)/shard_map/ppermute | solution.py:27
  130.8 7.4 %collective-permute-done.2 = f32[32,1280]{1,0:T(8,128)S(1)} collective-permute-done((f32[32,1280]{1,0:T(8,128)S(1)}, f32[32,1280]{1,0:T(8,128)S(1)}, u32[]{:S(2)}, u32[]{:S(2)}) %collective-permute-start.2) | collective-permute-done | bytes 163872 | tf_op jit(solution)/shard_map/ppermute | solution.py:27
  138.2 4.7 %collective-permute-start.3 = (f32[32,1280]{1,0:T(8,128)S(1)}, f32[32,1280]{1,0:T(8,128)S(1)}, u32[]{:S(2)}, u32[]{:S(2)}) collective-permute-start(f32[32,1280]{1,0:T(8,128)S(1)} %add.21), channel_id=1, source_target_pairs={{0,8},{1,9},{2,10},{3,11},{4,12},{5,13},{6,14},{7,15},{8,0},{9,1},... | collective-permute-start | bytes 491528 | tf_op jit(solution)/shard_map/ppermute | solution.py:27
  142.9 0.0 copy-done.1
  143.0 2.1 fusion.7
  145.0 7.7 %collective-permute-done.3 = f32[32,1280]{1,0:T(8,128)S(1)} collective-permute-done((f32[32,1280]{1,0:T(8,128)S(1)}, f32[32,1280]{1,0:T(8,128)S(1)}, u32[]{:S(2)}, u32[]{:S(2)}) %collective-permute-start.3) | collective-permute-done | bytes 163872 | tf_op jit(solution)/shard_map/ppermute | solution.py:27
  152.7 0.6 multiply_reduce_fusion
  153.4 74.1 %psum.7 = f32[]{:T(128)} all-reduce(f32[]{:T(128)} %get-tuple-element.2), channel_id=1, replica_groups=mesh['mod'=2,'loop'=16,'line'=16] {'mod','loop'}, use_global_device_ids=true, to_apply=%region_2.3 | all-reduce | flops 1 | bytes 8 | tf_op jit(solution)/shard_map/psum | solution.py:28
  228.2 0.7 multiply_bitcast_fusion
  (3 shorter events, 0.0 us)
Async XLA Ops:
  7.2 1.6 copy-start
  7.2 106.5 %reduce-scatter.2.cloned.1.call-start = ((), (), s32[]{:S(2)}) async-start(), calls=%async_computation.1 | async-start | bytes 2785280 | tf_op jit(solution)/shard_map/reduce_scatter | solution.py:17
  12.7 130.3 %copy-start.1 = (bf16[1,512,1280]{2,1,0:T(8,128)(2,1)S(1)}, bf16[1,512,1280]{2,1,0:T(8,128)(2,1)}, u32[]{:S(2)}) copy-start(bf16[1,512,1280]{2,1,0:T(8,128)(2,1)} %param.6) | copy-start | bytes 3932164
  113.7 3.5 %collective-permute-start = (f32[32,1280]{1,0:T(8,128)}, f32[32,1280]{1,0:T(8,128)S(1)}, u32[]{:S(2)}, u32[]{:S(2)}) collective-permute-start(f32[32,1280]{1,0:T(8,128)} %reduce-scatter.2.cloned.1.call-done), channel_id=1, source_target_pairs={{0,1},{1,0},{2,3},{3,2},{4,5},{5,4},{6,7},{7,6},{8,9},{9,8},{10,11... | collective-permute-start | bytes 491528 | tf_op jit(solution)/shard_map/ppermute | solution.py:27
  118.1 8.1 %collective-permute-start.1 = (f32[32,1280]{1,0:T(8,128)S(1)}, f32[32,1280]{1,0:T(8,128)S(1)}, u32[]{:S(2)}, u32[]{:S(2)}) collective-permute-start(f32[32,1280]{1,0:T(8,128)S(1)} %add.19), channel_id=1, source_target_pairs={{0,2},{1,3},{2,0},{3,1},{4,6},{5,7},{6,4},{7,5},{8,10},{9,11},{10,... | collective-permute-start | bytes 491528 | tf_op jit(solution)/shard_map/ppermute | solution.py:27
  126.3 12.0 %collective-permute-start.2 = (f32[32,1280]{1,0:T(8,128)S(1)}, f32[32,1280]{1,0:T(8,128)S(1)}, u32[]{:S(2)}, u32[]{:S(2)}) collective-permute-start(f32[32,1280]{1,0:T(8,128)S(1)} %add.20), channel_id=1, source_target_pairs={{0,4},{1,5},{2,6},{3,7},{4,0},{5,1},{6,2},{7,3},{8,12},{9,13},{10,... | collective-permute-start | bytes 491528 | tf_op jit(solution)/shard_map/ppermute | solution.py:27
  138.2 14.5 %collective-permute-start.3 = (f32[32,1280]{1,0:T(8,128)S(1)}, f32[32,1280]{1,0:T(8,128)S(1)}, u32[]{:S(2)}, u32[]{:S(2)}) collective-permute-start(f32[32,1280]{1,0:T(8,128)S(1)} %add.21), channel_id=1, source_target_pairs={{0,8},{1,9},{2,10},{3,11},{4,12},{5,13},{6,14},{7,15},{8,0},{9,1},... | collective-permute-start | bytes 491528 | tf_op jit(solution)/shard_map/ppermute | solution.py:27
Sparse Core Ops, SparseCore 0:
  12.8 100.7 reduce-scatter.1
